TPU v7x, 256 devices: a whole 4x4x8 slice. The times are simulated.
256 devices in a mesh: row: 16 (over z, y_hi), col: 16 (over x, y_lo, core).
Axes of the slice: x: 4, y: 4 (y_hi: 2, y_lo: 2; y = y_hi * 2 + y_lo), z: 8, core: 2. Of those that a mesh axis runs over, the one named last changes fastest.
Arguments:
- tokens: bfloat16 [1024, 14336], P('col', 'row'), may hold values from -6 to 6
- gate_weight: bfloat16 [14336, 26624], P('row', 'col'), may hold values from -0.046875 to 0.046875
- up_weight: bfloat16 [14336, 26624], P('row', 'col'), may hold values from -0.046875 to 0.046875
- upstream: bfloat16 [1024, 26624], P('row', 'col'), may hold values from -0.1875 to 0.1875
Outputs:
- grad_gate: bfloat16 [14336, 26624], P('row', 'col')
- grad_up: bfloat16 [14336, 26624], P('row', 'col')
All inputs are finite; a program needn't handle non-finite values.
Results may differ from a plain program's by a relative error of at most 0.005.
Values may be sent and summed in bfloat16 or wider, within the bound.
A program may use at most 128 MiB of HBM per device.

v0:
```python
import jax
import jax.numpy as jnp
from jax import lax
from jax.sharding import PartitionSpec as P


def swiglu_grads(preacts, cotangent_rows, hidden_cols):
    gate_pre = preacts[:, :hidden_cols]
    up_pre = preacts[:, hidden_cols:]
    squash = jax.nn.sigmoid(gate_pre)
    cotangent = cotangent_rows.astype(jnp.float32)
    d_up = cotangent * gate_pre * squash
    d_gate = cotangent * up_pre * squash * (1.0 + gate_pre * (1.0 - squash))
    return jnp.concatenate([d_gate, d_up], axis=1).astype(jnp.bfloat16)


def local(tokens, gate_weight, up_weight, upstream):
    hidden_cols = gate_weight.shape[1]
    numbers = (((0,), (0,)), ((), ()))
    weights = jnp.concatenate([gate_weight, up_weight], axis=1)
    gathered = lax.all_gather(tokens, "col", axis=0, tiled=True)
    partial_pre = jnp.dot(gathered, weights, preferred_element_type=jnp.float32)
    preacts = lax.psum(partial_pre, "row")
    cotangent_all = lax.all_gather(upstream, "row", axis=0, tiled=True)
    gradients = swiglu_grads(preacts, cotangent_all, hidden_cols)
    weight_grads = lax.dot_general(gathered, gradients, numbers, preferred_element_type=jnp.float32)
    rounded = weight_grads.astype(jnp.bfloat16)
    return (rounded[:, :hidden_cols], rounded[:, hidden_cols:])


def solution(mesh):
    return jax.shard_map(
        local,
        mesh=mesh,
        in_specs=(P("col", "row"), P("row", "col"), P("row", "col"), P("row", "col")),
        out_specs=(P("row", "col"), P("row", "col")),
        check_vma=False,
    )
```

profile of v0, /device:TPU:97, one launch (start us, length us, event | category | flops | bytes accessed | tf_op | source)
XLA Modules:
  0.0 766.3 jit_solution(7752807111683964820)
XLA Ops:
  7.2 0.0 all-gather.5.cloned.1.call-start
  7.2 0.7 all-gather.5.cloned.1.call-update
  7.9 0.0 all-gather.3.cloned.1.call-start
  7.9 0.7 all-gather.3.cloned.1.call-update
  8.6 0.0 all-reduce.2.cloned.1.call-start
  8.7 39.3 %all-gather.5.cloned.1.call-done = bf16[1024,896]{1,0:T(8,128)(2,1)} async-done(((bf16[64,896]{1,0:T(8,128)(2,1)}), bf16[1024,896]{1,0:T(8,128)(2,1)}) %all-gather.5.cloned.1.call-update) | async-done | bytes 1835024 | tf_op jit(solution)/shard_map/all_gather | solution.py:21
  48.0 13.5 %convolution_bitcast_fusion = f32[1024,3328]{0,1:T(8,128)} fusion(bf16[1024,896]{1,0:T(8,128)(2,1)} %all-gather.5.cloned.1.call-done, bf16[896,1664]{1,0:T(8,128)(2,1)} %param.6, bf16[896,1664]{1,0:T(8,128)(2,1)} %param.5), kind=kOutput, calls=%fused_computation | convolution fusion | flops 6118834176 | bytes 21430272 | tf_op jit(solution)/shard_map/dot_general | solution.py:22
  61.5 0.0 all-reduce.2.cloned.1.call-update
  61.5 78.7 %all-gather.3.cloned.1.call-done = bf16[1024,1664]{1,0:T(8,128)(2,1)} async-done(((bf16[64,1664]{1,0:T(8,128)(2,1)}), bf16[1024,1664]{1,0:T(8,128)(2,1)}) %all-gather.3.cloned.1.call-update) | async-done | bytes 3407888 | tf_op jit(solution)/shard_map/all_gather | solution.py:24
  140.3 4.2 copy.9
  144.5 586.7 %all-reduce.2.cloned.1.call-done = f32[1024,3328]{0,1:T(8,128)} async-done(((f32[1024,3328]{0,1:T(8,128)}), f32[1024,3328]{0,1:T(8,128)}) %all-reduce.2.cloned.1.call-update) | async-done | bytes 13631504 | tf_op jit(solution)/shard_map/psum | solution.py:23
  731.2 0.0 copy-start
  731.2 6.7 fusion.2
  737.9 0.0 copy-done
  737.9 10.8 %fusion.8 = bf16[896,3328]{0,1:T(8,128)(2,1)S(1)} fusion(bf16[1024,896]{1,0:T(8,128)(2,1)S(1)} %copy-done, bf16[1024,1664]{0,1:T(8,128)(2,1)S(1)} %get-tuple-element.7, bf16[1024,1664]{0,1:T(8,128)(2,1)S(1)} %get-tuple-element.6), kind=kOutput, calls=%fused_computation.13 | convolution fusion | flops 6123520000 | bytes 14614528 | tf_op jit(solution)/shard_map/dot_general | solution.py:26
  748.8 2.1 fusion.16
  750.8 5.4 copy.10
  756.2 3.5 copy.11
Async XLA Ops:
  7.2 40.8 %all-gather.5.cloned.1.call-start = ((), (), s32[]{:S(2)}) async-start(), calls=%async_computation.1 | async-start | bytes 1949696 | tf_op jit(solution)/shard_map/all_gather | solution.py:21
  7.9 132.4 %all-gather.3.cloned.1.call-start = ((), (), s32[]{:S(2)}) async-start(), calls=%async_computation | async-start | bytes 3620864 | tf_op jit(solution)/shard_map/all_gather | solution.py:24
  8.6 722.5 %all-reduce.2.cloned.1.call-start = ((), (), s32[]{:S(2)}) async-start(), calls=%async_computation.2 | async-start | bytes 27262976 | tf_op jit(solution)/shard_map/psum | solution.py:23
  731.2 6.7 copy-start
Sparse Core Ops, SparseCore 0:
  9.8 38.1 all-gather.4
  50.6 89.6 all-gather.2
  143.0 588.1 all-reduce.1
where the time goes:
time: 767 us; the launch traced here: 766 us
  waiting for transfers between devices  706 us (92%)
  matrix products  24.4 us (3%)
  local copies, waits for them, and re-layouts  15.2 us (2%)
  between operations  13.8 us (2%)
    psum x1, waiting for transfers between devices, local(): preacts = lax.psum(partial_pre, 'row')  587 us
    all_gather x1, waiting for transfers between devices, local(): cotangent_all = lax.all_gather(upstream, 'row', axis=0, tiled=True)  78.7 us
    all_gather x1, waiting for transfers between devices, local(): gathered = lax.all_gather(tokens, 'col', axis=0, tiled=True)  39.3 us
  transfers between devices with their start and end apart: 3, of which 3 were waited for; matrix products, arithmetic and copies ran while one was open for 2% of the time, Pallas kernels for 0%

commit v1 on v0

--- a/solution.py
+++ b/solution.py
@@ -21,7 +21,9 @@
     gathered = lax.all_gather(tokens, "col", axis=0, tiled=True)
     partial_pre = jnp.dot(gathered, weights, preferred_element_type=jnp.float32)
     preacts = lax.psum(partial_pre, "row")
-    cotangent_all = lax.all_gather(upstream, "row", axis=0, tiled=True)
+    cotangent_all = jnp.concatenate(
+        lax.all_to_all(jnp.stack([upstream] * lax.axis_size("row")), "row", 0, 0), axis=0
+    )
     gradients = swiglu_grads(preacts, cotangent_all, hidden_cols)
     weight_grads = lax.dot_general(gathered, gradients, numbers, preferred_element_type=jnp.float32)
     rounded = weight_grads.astype(jnp.bfloat16)

time: 767 us -> 719 us (0.937)
  waiting for transfers between devices: 706 us -> 530 us
  blocking collectives: 0 us -> 119 us
    all_to_all x0 -> x1, blocking collectives: none -> 119 us  [local(): lax.all_to_all(jnp.stack([upstream] * lax.axis_size('row')), 'row', 0, 0)]
    psum x1, waiting for transfers between devices: 587 us -> 489 us  [local(): preacts = lax.psum(partial_pre, 'row')]
    all_gather x1 -> x0, waiting for transfers between devices: 78.7 us -> none  [local(): cotangent_all = lax.all_gather(upstream, 'row', axis=0, tiled=True)]
  transfers between devices with their start and end apart: 3 -> 2, of which waited for: 3 -> 2; matrix products, arithmetic and copies ran while one was open for 2% -> 2% of each run, Pallas kernels for 0% -> 0%
where the time goes in v1:
time: 719 us
  waiting for transfers between devices  530 us (74%)
  blocking collectives  119 us (17%)
  matrix products  24.3 us (3%)
  local copies, waits for them, and re-layouts  19.9 us (3%)
  between operations  14.1 us (2%)
  other arithmetic  12.4 us (2%)
    psum x1, waiting for transfers between devices, local(): preacts = lax.psum(partial_pre, 'row')  489 us
    all_to_all x1, blocking collectives, local(): lax.all_to_all(jnp.stack([upstream] * lax.axis_size('row')), 'row', 0, 0)  119 us
    all_gather x1, waiting for transfers between devices, local(): gathered = lax.all_gather(tokens, 'col', axis=0, tiled=True)  40.1 us
  transfers between devices with their start and end apart: 2, of which 2 were waited for; matrix products, arithmetic and copies ran while one was open for 2% of the time, Pallas kernels for 0%

profile of v1, /device:TPU:97, one launch (start us, length us, event | category | flops | bytes accessed | tf_op | source)
XLA Modules:
  0.0 719.0 jit_solution(14863140185444737853)
XLA Ops:
  7.2 0.0 all-gather.2.cloned.1.call-start
  7.2 0.7 all-gather.2.cloned.1.call-update
  7.9 0.0 all-reduce.2.cloned.1.call-start
  7.9 40.1 %all-gather.2.cloned.1.call-done = bf16[1024,896]{1,0:T(8,128)(2,1)} async-done(((bf16[64,896]{1,0:T(8,128)(2,1)}), bf16[1024,896]{1,0:T(8,128)(2,1)}) %all-gather.2.cloned.1.call-update) | async-done | bytes 1835024 | tf_op jit(solution)/shard_map/all_gather | solution.py:21
  48.0 13.5 %convolution_bitcast_fusion = f32[1024,3328]{0,1:T(8,128)} fusion(bf16[1024,896]{1,0:T(8,128)(2,1)} %all-gather.2.cloned.1.call-done, bf16[896,1664]{1,0:T(8,128)(2,1)} %param.6, bf16[896,1664]{1,0:T(8,128)(2,1)} %param.5), kind=kOutput, calls=%fused_computation | convolution fusion | flops 6118834176 | bytes 21430272 | tf_op jit(solution)/shard_map/dot_general | solution.py:22
  61.5 0.0 copy-start
  61.5 0.0 all-reduce.2.cloned.1.call-update
  61.6 0.9 copy-done
  62.5 0.4 stack.2
  62.8 118.6 %all_to_all.5 = bf16[16,64,1664]{2,1,0:T(8,128)(2,1)S(1)} all-to-all(bf16[16,64,1664]{2,1,0:T(8,128)(2,1)S(1)} %stack.2), channel_id=1, replica_groups=mesh['row'=16,'col'=16] {'row'}, dimensions={0} | all-to-all | bytes 6815744 | tf_op jit(solution)/shard_map/all_to_all | solution.py:25
  181.4 3.5 bitcast_convert_fusion
  184.9 7.6 %copy.9 = f32[1024,1664]{0,1:T(8,128)} copy(f32[1024,1664]{1,0:T(8,128)} %bitcast_convert_fusion) | data formatting | bytes 13631488 | tf_op jit(solution)/shard_map/convert_element_type | solution.py:11
  192.5 0.0 copy-start.1
  192.5 489.0 %all-reduce.2.cloned.1.call-done = f32[1024,3328]{0,1:T(8,128)} async-done(((f32[1024,3328]{0,1:T(8,128)}), f32[1024,3328]{0,1:T(8,128)}) %all-reduce.2.cloned.1.call-update) | async-done | bytes 13631504 | tf_op jit(solution)/shard_map/psum | solution.py:23
  681.5 8.9 %fusion.2 = (bf16[1024,1664]{0,1:T(8,128)(2,1)S(1)}, bf16[1024,1664]{0,1:T(8,128)(2,1)S(1)}) fusion(f32[1024,1664]{0,1:T(8,128)} %copy.9, f32[1024,3328]{0,1:T(8,128)} %all-reduce.2.cloned.1.call-done), kind=kLoop, calls=%fused_computation.5 | loop fusion | flops 22151168 | bytes 27262976 | tf_op jit(solution)/shard_map/convert.1
  690.4 0.0 copy-done.1
  690.4 10.8 %fusion.6 = bf16[896,3328]{0,1:T(8,128)(2,1)S(1)} fusion(bf16[1024,896]{1,0:T(8,128)(2,1)S(1)} %copy-done.1, bf16[1024,1664]{0,1:T(8,128)(2,1)S(1)} %get-tuple-element.7, bf16[1024,1664]{0,1:T(8,128)(2,1)S(1)} %get-tuple-element.6), kind=kOutput, calls=%fused_computation.11 | convolution fusion | flops 6123520000 | bytes 14614528 | tf_op jit(solution)/shard_map/dot_general | solution.py:28
  701.2 2.1 fusion.14
  703.3 5.4 copy.11
  708.6 3.5 copy.12
Async XLA Ops:
  7.2 40.8 %all-gather.2.cloned.1.call-start = ((), (), s32[]{:S(2)}) async-start(), calls=%async_computation.1 | async-start | bytes 1949696 | tf_op jit(solution)/shard_map/all_gather | solution.py:21
  7.9 673.6 %all-reduce.2.cloned.1.call-start = ((), (), s32[]{:S(2)}) async-start(), calls=%async_computation.2 | async-start | bytes 27262976 | tf_op jit(solution)/shard_map/psum | solution.py:23
  61.5 0.9 copy-start
  192.5 497.9 %copy-start.1 = (bf16[1024,896]{1,0:T(8,128)(2,1)S(1)}, bf16[1024,896]{1,0:T(8,128)(2,1)}, u32[]{:S(2)}) copy-start(bf16[1024,896]{1,0:T(8,128)(2,1)} %all-gather.2.cloned.1.call-done) | copy-start | bytes 5505028
Sparse Core Ops, SparseCore 0:
  9.8 38.1 all-gather.1
  61.7 619.7 all-reduce.1
